TPU v7x, 32 devices: a whole 2x2x4 slice. The times are simulated.
32 devices in a mesh: scen: 4 (over y, x), opt: 8 (over z, core).
Axes of the slice: x: 2, y: 2, z: 4, core: 2. Of those that a mesh axis runs over, the one named last changes fastest.
Arguments:
- option_coefs: float32 [4096, 1024], P(('opt', 'scen')), may hold values from -0.75 to 0.75
- underlying_of: int32 [4096, 1], P('opt'), may hold values from 0 to 31; in each aligned block of 128 rows (0 to 127, 128 to 255, ...) at most 8 rows name the same one
- log_return_mean: float32 [32, 1024], P(('scen', 'opt')), may hold values from -1 to 1
- log_return_spread: float32 [32, 1024], P(('scen', 'opt')), may hold values from 1e-06 to 0.0001
- cost: float32 [4096], P('opt'), may hold values from -3 to 3
- positions: float32 [4096], P('opt'), may hold values from -1 to 1
- base_loss: float32 [1024], P('scen'), may hold values from -6 to 6
- duals: float32 [1024], P('scen'), may hold values from 0 to 1
- threshold: float32 [1], replicated, may hold values from -2 to 2
Outputs:
- scenario_values: float32 [4096, 1024], P('opt', 'scen')
- new_positions: float32 [4096], P('opt')
- new_duals: float32 [1024], P('scen')
- new_threshold: float32 [1], replicated
Inputs may be any that keep to these rules, and one draw needn't show every extreme that they name: `underlying_of`: in each aligned block of 128 options no underlying is named more than 8 times, a bound that some block reaches; every underlying is named somewhere.
All inputs are finite; a program needn't handle non-finite values.
Results may differ from a plain program's by a relative error of at most 0.0003.
Values sent between devices are 32-bit elements; how exact they have to be, the bound alone decides.
A program may use at most 64 MiB of HBM per device.

v0:
```python
import math
import jax
import jax.numpy as jnp
from jax import lax
from jax.sharding import PartitionSpec as P

ITERS = 2
LOW_END = -4.0
HIGH_END = 4.0
TAIL_LEVEL = 0.9
PRIMAL_STEP = 0.5
THRESH_STEP = 0.05
DUAL_STEP = 0.5


def cosine_terms(drift_rows, variance_rows, term_count):
    frequency = jnp.arange(term_count, dtype=jnp.float32) * (math.pi / (HIGH_END - LOW_END))
    weight = jnp.where(jnp.arange(term_count) == 0, 0.5, 1.0).astype(jnp.float32) * (
        2.0 / (HIGH_END - LOW_END)
    )
    decay = jnp.exp(-0.5 * variance_rows[:, None] * frequency * frequency)
    return weight * decay * jnp.cos(frequency * (drift_rows[:, None] - LOW_END))


def slot_ranks(owners, label_count):
    onehot = (owners[..., None] == jnp.arange(label_count, dtype=jnp.int32)).astype(jnp.int32)
    before = jnp.cumsum(onehot, axis=1) - onehot
    return jnp.sum(before * onehot, axis=-1)


def on_device(
    option_coefs,
    underlying_of,
    log_return_mean,
    log_return_spread,
    cost,
    positions,
    base_loss,
    duals,
    threshold,
):
    outcome_total = lax.axis_size("scen")
    opt_count = lax.axis_size("opt")
    processor_total = outcome_total * opt_count
    my_row = lax.axis_index("scen")
    block_rows = option_coefs.shape[0]
    term_count = option_coefs.shape[1]
    outcome_lines = duals.shape[0]
    total_scen = log_return_mean.shape[1]
    place_limit = max(2, 2 * block_rows // processor_total)
    column_owner = underlying_of[:, 0].reshape(outcome_total, block_rows)
    column_rank = slot_ranks(column_owner, processor_total)
    my_owner = lax.dynamic_index_in_dim(column_owner, my_row, 0, keepdims=False)
    my_rank = lax.dynamic_index_in_dim(column_rank, my_row, 0, keepdims=False)
    outgoing = jnp.zeros((processor_total * place_limit, term_count), jnp.float32)
    outgoing = outgoing.at[my_owner * place_limit + my_rank].set(option_coefs)
    incoming = lax.all_to_all(
        outgoing.reshape(processor_total, place_limit, term_count),
        ("scen", "opt"),
        split_axis=0,
        concat_axis=0,
        tiled=True,
    )
    incoming = incoming.reshape(outcome_total, opt_count, place_limit, term_count)
    contraction = "abmk,sk->bams"
    holding_buffer_dims = (outcome_total, opt_count, outcome_total, place_limit, outcome_lines)

    def contract_cost_tile(cost_tile_number, valued_contracts):
        drift_rows = lax.dynamic_slice_in_dim(
            log_return_mean[0], cost_tile_number * outcome_lines, outcome_lines
        )
        variance_rows = lax.dynamic_slice_in_dim(
            log_return_spread[0], cost_tile_number * outcome_lines, outcome_lines
        )
        cosine_table = cosine_terms(drift_rows, variance_rows, term_count)
        contract_worths = jnp.einsum(
            contraction, incoming, cosine_table, precision=lax.Precision.HIGHEST
        )
        return lax.dynamic_update_index_in_dim(
            valued_contracts, contract_worths, cost_tile_number, 0
        )

    valued_contracts = lax.fori_loop(
        0, outcome_total, contract_cost_tile, jnp.zeros(holding_buffer_dims, jnp.float32)
    )
    arrived = lax.all_to_all(
        valued_contracts.reshape(processor_total, outcome_total, place_limit, outcome_lines),
        ("scen", "opt"),
        split_axis=0,
        concat_axis=0,
        tiled=True,
    )
    flat_index = (
        column_owner * outcome_total + jnp.arange(outcome_total, dtype=jnp.int32)[:, None]
    ) * place_limit + column_rank
    local_tile = jnp.take(
        arrived.reshape(processor_total * outcome_total * place_limit, outcome_lines),
        flat_index.reshape(-1),
        axis=0,
    )
    root_scen = math.sqrt(total_scen)
    root_opt = math.sqrt(opt_count * local_tile.shape[0])
    tail_mass = (1.0 - TAIL_LEVEL) * total_scen
    holding = positions
    weights = duals
    level = threshold[0]
    for iteration in range(ITERS):
        part_gradient = jnp.dot(local_tile, weights, precision=lax.Precision.HIGHEST)
        gradient_sum, dual_mass = lax.psum((part_gradient, jnp.sum(weights)), "scen")
        holding_next = jnp.clip(
            holding - PRIMAL_STEP * (cost - gradient_sum / root_scen), -1.0, 1.0
        )
        level_next = level - THRESH_STEP * (1.0 - dual_mass / tail_mass)
        holding_bar = 2.0 * holding_next - holding
        level_bar = 2.0 * level_next - level
        part_pnl = jnp.dot(holding_bar, local_tile, precision=lax.Precision.HIGHEST)
        pnl = lax.psum(part_pnl, "opt") / root_opt
        weights = jnp.clip(weights + DUAL_STEP * (base_loss - pnl - level_bar), 0.0, 1.0)
        holding = holding_next
        level = level_next
    return (local_tile, holding, weights, level.reshape(1))


def solution(mesh):
    in_specs = (
        P(("opt", "scen"), None),
        P("opt", None),
        P(("scen", "opt"), None),
        P(("scen", "opt"), None),
        P("opt"),
        P("opt"),
        P("scen"),
        P("scen"),
        P(),
    )
    out_specs = (P("opt", "scen"), P("opt"), P("scen"), P())
    return jax.shard_map(
        on_device, mesh=mesh, in_specs=in_specs, out_specs=out_specs, check_vma=False
    )
```

profile of v0, /device:TPU:0, one launch (start us, length us, event | category | flops | bytes accessed | tf_op | source)
XLA Modules:
  0.0 147.9 jit_solution(6425001164244018007)
XLA Ops:
  0.6 0.0 copy-start.1
  0.6 0.7 copy-done.1
  1.3 0.1 fusion.14
  1.5 0.3 reduce_window_sum.11
  1.7 0.2 select_reduce_fusion
  2.0 2.6 %scatter_custom_fusion = f32[256,1024]{1,0:T(8,128)} fusion(s32[128]{0:T(128)S(1)} %fusion.15, f32[128,1024]{1,0:T(8,128)} %param.11, f32[]{:T(128)} %constant.174.clone.1), kind=kCustom, calls=%fused_computation.21 | custom fusion | bytes 1049088 | tf_op jit(solution)/shard_map/scatter | solution.py:56
  4.6 7.3 %all-to-all-start = ((f32[32,8,1024]{2,1,0:T(8,128)}), f32[32,8,1024]{2,1,0:T(8,128)S(1)}, u32[]{:S(2)}, u32[]{:S(2)}) async-start(f32[32,8,1024]{2,1,0:T(8,128)} %bitcast.11), calls=%async_computation | async-start | bytes 2097152 | tf_op jit(solution)/shard_map/all_to_all | solution.py:57
  11.9 27.5 %all-to-all-done = f32[32,8,1024]{2,1,0:T(8,128)S(1)} async-done(((f32[32,8,1024]{2,1,0:T(8,128)}), f32[32,8,1024]{2,1,0:T(8,128)S(1)}, u32[]{:S(2)}, u32[]{:S(2)}) %all-to-all-start) | async-done | bytes 1048608 | tf_op jit(solution)/shard_map/all_to_all | solution.py:57
  39.4 24.5 %while.15 = (s32[]{:T(128)}, f32[4,8,4,8,256]{4,3,2,1,0:T(8,128)}, f32[1,1024]{1,0:T(1,128)}, f32[1,1024]{1,0:T(1,128)}, f32[4,8,8,1024]{3,2,1,0:T(8,128)S(1)}, ...) while((s32[]{:T(128)}, f32[4,8,4,8,256]{4,3,2,1,0:T(8,128)}, f32[1,1024]{1,0:T(1,128)}, ...), condition=%wide.region_4.5_spmd, body=%wide.region_3.4_spmd.sunk | while | flops 806621696 | bytes 1858191 | solution.py:83
  39.4 0.7 dynamic-slice_add_fusion.2
  40.1 4.7 %convolution_bitcast_fusion.2 = f32[1,8,4,8,256]{4,3,1,2,0:T(8,128)S(1)} fusion(f32[4,8,8,1024]{3,2,1,0:T(8,128)S(1)} %get-tuple-element.222, f32[256]{0:T(256)S(1)} %bitcast.56, f32[1024]{0:T(1024)S(1)} %get-tuple-element.197, f32[256]{0:T(256)S(1)} %bitcast.57, f32[1024]{0:T(1024)S(1)} %get-tuple-element.199), kind=kOutput, calls=%fused_computation.2.clone.1 | convolution fusion | flops 806617088 | bytes 1320960 | tf_op jit(solution)/shard_map/while/body/eval_jaxpr/abmk,sk->bams/dot_general | solution.py:76
  44.8 0.7 copy_dynamic-update-slice_fusion.2
  45.5 0.7 dynamic-slice_add_fusion.2
  46.2 4.7 %convolution_bitcast_fusion.2 = f32[1,8,4,8,256]{4,3,1,2,0:T(8,128)S(1)} fusion(f32[4,8,8,1024]{3,2,1,0:T(8,128)S(1)} %get-tuple-element.222, f32[256]{0:T(256)S(1)} %bitcast.56, f32[1024]{0:T(1024)S(1)} %get-tuple-element.197, f32[256]{0:T(256)S(1)} %bitcast.57, f32[1024]{0:T(1024)S(1)} %get-tuple-element.199), kind=kOutput, calls=%fused_computation.2.clone.1 | convolution fusion | flops 806617088 | bytes 1320960 | tf_op jit(solution)/shard_map/while/body/eval_jaxpr/abmk,sk->bams/dot_general | solution.py:76
  50.9 0.7 copy_dynamic-update-slice_fusion.2
  51.6 0.7 dynamic-slice_add_fusion.2
  52.3 4.7 %convolution_bitcast_fusion.2 = f32[1,8,4,8,256]{4,3,1,2,0:T(8,128)S(1)} fusion(f32[4,8,8,1024]{3,2,1,0:T(8,128)S(1)} %get-tuple-element.222, f32[256]{0:T(256)S(1)} %bitcast.56, f32[1024]{0:T(1024)S(1)} %get-tuple-element.197, f32[256]{0:T(256)S(1)} %bitcast.57, f32[1024]{0:T(1024)S(1)} %get-tuple-element.199), kind=kOutput, calls=%fused_computation.2.clone.1 | convolution fusion | flops 806617088 | bytes 1320960 | tf_op jit(solution)/shard_map/while/body/eval_jaxpr/abmk,sk->bams/dot_general | solution.py:76
  57.0 0.7 copy_dynamic-update-slice_fusion.2
  57.7 0.7 dynamic-slice_add_fusion.2
  58.5 4.7 %convolution_bitcast_fusion.2 = f32[1,8,4,8,256]{4,3,1,2,0:T(8,128)S(1)} fusion(f32[4,8,8,1024]{3,2,1,0:T(8,128)S(1)} %get-tuple-element.222, f32[256]{0:T(256)S(1)} %bitcast.56, f32[1024]{0:T(1024)S(1)} %get-tuple-element.197, f32[256]{0:T(256)S(1)} %bitcast.57, f32[1024]{0:T(1024)S(1)} %get-tuple-element.199), kind=kOutput, calls=%fused_computation.2.clone.1 | convolution fusion | flops 806617088 | bytes 1320960 | tf_op jit(solution)/shard_map/while/body/eval_jaxpr/abmk,sk->bams/dot_general | solution.py:76
  63.1 0.7 copy_dynamic-update-slice_fusion.2
  63.9 0.0 copy-start.2
  63.9 2.8 %all-to-all-start.1 = ((f32[32,4,8,256]{3,2,1,0:T(8,128)}), f32[32,4,8,256]{3,2,1,0:T(8,128)S(1)}, u32[]{:S(2)}, u32[]{:S(2)}) async-start(f32[32,4,8,256]{3,2,1,0:T(8,128)} %bitcast.13), calls=%async_computation.1 | async-start | bytes 2097152 | tf_op jit(solution)/shard_map/all_to_all | solution.py:86
  66.7 0.0 copy-done.2
  66.7 0.6 reduce_sum.31
  68.0 26.2 %all-to-all-done.1 = f32[32,4,8,256]{3,2,1,0:T(8,128)S(1)} async-done(((f32[32,4,8,256]{3,2,1,0:T(8,128)}), f32[32,4,8,256]{3,2,1,0:T(8,128)S(1)}, u32[]{:S(2)}, u32[]{:S(2)}) %all-to-all-start.1) | async-done | bytes 1048608 | tf_op jit(solution)/shard_map/all_to_all | solution.py:86
  94.1 1.6 %gather_fusion = f32[512,256]{1,0:T(8,128)S(1)} fusion(f32[1024,256]{1,0:T(8,128)S(1)} %bitcast.54, s32[1024]{0:T(1024)S(1)} %pad_clamp_fusion), kind=kCustom, calls=%fused_computation | custom fusion | bytes 1050624 | tf_op jit(solution)/shard_map/jit(_take)/gather | solution.py:96
  95.7 0.1 broadcast_select_fusion
  95.9 0.0 copy-start
  95.9 0.5 fusion.17
  96.4 0.0 copy-start.3
  96.4 0.0 copy-start.4
  96.4 8.7 %all-reduce.1 = (f32[512]{0:T(512)S(1)}, f32[]{:T(128)}) all-reduce(f32[512]{0:T(512)S(1)} %bitcast.65, f32[]{:T(128)} %reduce_sum.31), channel_id=1, replica_groups=mesh['scen'=4,'opt'=8] {'scen'}, use_global_device_ids=true, to_apply=%region_5.6 | all-reduce | flops 513 | bytes 4104 | tf_op jit(solution)/shard_map/psum | solution.py:109
  105.1 0.0 copy-done.3
  105.1 0.0 copy-done.4
  105.1 0.3 fusion.18
  105.4 13.6 %psum.43 = f32[256]{0:T(256)S(1)} all-reduce(f32[256]{0:T(256)S(1)} %bitcast.70), channel_id=1, replica_groups=mesh['scen'=4,'opt'=8] {'opt'}, use_global_device_ids=true, to_apply=%region_6.7 | all-reduce | flops 256 | bytes 2048 | tf_op jit(solution)/shard_map/psum | solution.py:117
  119.7 0.0 copy-start.5
  119.7 0.7 copy-done.5
  120.3 0.6 fusion.16
  120.9 0.5 fusion.19
  121.5 9.6 %all-reduce = (f32[512]{0:T(512)S(1)}, f32[]{:T(128)}) all-reduce(f32[512]{0:T(512)S(1)} %bitcast.64, f32[]{:T(128)} %get-tuple-element.153), channel_id=1, replica_groups=mesh['scen'=4,'opt'=8] {'scen'}, use_global_device_ids=true, to_apply=%region_9.10 | all-reduce | flops 513 | bytes 4104 | tf_op jit(solution)/shard_map/psum | solution.py:109
  131.7 0.6 multiply_subtract_fusion
  132.3 0.0 copy-done
  132.3 0.3 fusion.20
  132.6 13.6 %psum.46 = f32[256]{0:T(256)S(1)} all-reduce(f32[256]{0:T(256)S(1)} %bitcast.71), channel_id=1, replica_groups=mesh['scen'=4,'opt'=8] {'opt'}, use_global_device_ids=true, to_apply=%region_10.11 | all-reduce | flops 256 | bytes 2048 | tf_op jit(solution)/shard_map/psum | solution.py:117
  146.2 0.6 add_clamp_fusion
  (10 shorter events, 0.1 us)
Async XLA Ops:
  0.6 0.7 copy-start.1
  4.6 34.8 %all-to-all-start = ((f32[32,8,1024]{2,1,0:T(8,128)}), f32[32,8,1024]{2,1,0:T(8,128)S(1)}, u32[]{:S(2)}, u32[]{:S(2)}) async-start(f32[32,8,1024]{2,1,0:T(8,128)} %bitcast.11), calls=%async_computation | async-start | bytes 2097152 | tf_op jit(solution)/shard_map/all_to_all | solution.py:57
  63.9 2.8 %copy-start.2 = (f32[256]{0:T(256)S(1)}, f32[256]{0:T(256)}, u32[]{:S(2)}) copy-start(f32[256]{0:T(256)} %param.18) | copy-start | bytes 3076
  63.9 30.3 %all-to-all-start.1 = ((f32[32,4,8,256]{3,2,1,0:T(8,128)}), f32[32,4,8,256]{3,2,1,0:T(8,128)S(1)}, u32[]{:S(2)}, u32[]{:S(2)}) async-start(f32[32,4,8,256]{3,2,1,0:T(8,128)} %bitcast.13), calls=%async_computation.1 | async-start | bytes 2097152 | tf_op jit(solution)/shard_map/all_to_all | solution.py:86
  95.9 36.4 %copy-start = (f32[512,256]{1,0:T(8,128)}, f32[512,256]{1,0:T(8,128)S(1)}, u32[]{:S(2)}) copy-start(f32[512,256]{1,0:T(8,128)S(1)} %broadcast_select_fusion) | copy-start | bytes 1572868
  96.4 8.7 %copy-start.3 = (f32[512]{0:T(512)S(1)}, f32[512]{0:T(512)}, u32[]{:S(2)}) copy-start(f32[512]{0:T(512)} %param.16) | copy-start | bytes 6148
  96.4 8.7 %copy-start.4 = (f32[512]{0:T(512)S(1)}, f32[512]{0:T(512)}, u32[]{:S(2)}) copy-start(f32[512]{0:T(512)} %param.15) | copy-start | bytes 6148
  119.7 0.7 copy-start.5
where the time goes:
time: 148 us
  waiting for transfers between devices  53.6 us (36%)
  blocking collectives  45.5 us (31%)
  matrix products  20.4 us (14%)
  starting transfers between devices  10.1 us (7%)
  local copies, waits for them, and re-layouts  8.42 us (6%)
  other arithmetic  6.02 us (4%)
  between operations  3.86 us (3%)
    all_to_all x1, waiting for transfers between devices, on_device(): lax.all_to_all(outgoing.reshape(processor_total, place_limit, term_count)...  27.5 us
    psum x2, blocking collectives, on_device(): pnl = lax.psum(part_pnl, 'opt') / root_opt  27.3 us
    all_to_all x1, waiting for transfers between devices, on_device(): lax.all_to_all(valued_contracts.reshape(processor_total, outcome_total, p...  26.2 us
    dot_general x4, matrix products, contract_cost_tile(): jnp.einsum(contraction, incoming, cosine_table, precision=lax.Precision.H...  18.8 us
    psum x2, blocking collectives, on_device(): lax.psum((part_gradient, jnp.sum(weights)), 'scen')  18.2 us
    all_to_all x1, starting transfers between devices, on_device(): lax.all_to_all(outgoing.reshape(processor_total, place_limit, term_count)...  7.33 us
  transfers between devices with their start and end apart: 2, of which 2 were waited for; matrix products, arithmetic and copies ran while one was open for 0% of the time, Pallas kernels for 0%

commit v1 on v0

--- a/solution.py
+++ b/solution.py
@@ -11,6 +11,11 @@
 PRIMAL_STEP = 0.5
 THRESH_STEP = 0.05
 DUAL_STEP = 0.5
+
+
+def gather_and_add(array, mesh_axis):
+    terms = lax.all_gather(array, mesh_axis)
+    return jnp.sum(terms, axis=0)
 
 
 def cosine_terms(drift_rows, variance_rows, term_count):
@@ -114,7 +119,7 @@
         holding_bar = 2.0 * holding_next - holding
         level_bar = 2.0 * level_next - level
         part_pnl = jnp.dot(holding_bar, local_tile, precision=lax.Precision.HIGHEST)
-        pnl = lax.psum(part_pnl, "opt") / root_opt
+        pnl = gather_and_add(part_pnl, "opt") / root_opt
         weights = jnp.clip(weights + DUAL_STEP * (base_loss - pnl - level_bar), 0.0, 1.0)
         holding = holding_next
         level = level_next

time: 148 us -> 140 us (0.946)
  blocking collectives: 45.5 us -> 37.1 us
    psum x2 -> x0, blocking collectives: 27.3 us -> none  [on_device(): pnl = lax.psum(part_pnl, 'opt') / root_opt]
    all_gather x0 -> x2, blocking collectives: none -> 19.9 us  [gather_and_add(): terms = lax.all_gather(array, mesh_axis)]
where the time goes in v1:
time: 140 us
  waiting for transfers between devices  53.6 us (38%)
  blocking collectives  37.1 us (26%)
  matrix products  20.4 us (15%)
  starting transfers between devices  10.1 us (7%)
  local copies, waits for them, and re-layouts  8.42 us (6%)
  other arithmetic  6.07 us (4%)
  between operations  3.86 us (3%)
    all_to_all x1, waiting for transfers between devices, on_device(): lax.all_to_all(outgoing.reshape(processor_total, place_limit, term_count)...  27.5 us
    all_to_all x1, waiting for transfers between devices, on_device(): lax.all_to_all(valued_contracts.reshape(processor_total, outcome_total, p...  26.2 us
    all_gather x2, blocking collectives, gather_and_add(): terms = lax.all_gather(array, mesh_axis)  19.9 us
    dot_general x4, matrix products, contract_cost_tile(): jnp.einsum(contraction, incoming, cosine_table, precision=lax.Precision.H...  18.8 us
    psum x2, blocking collectives, on_device(): lax.psum((part_gradient, jnp.sum(weights)), 'scen')  17.2 us
    all_to_all x1, starting transfers between devices, on_device(): lax.all_to_all(outgoing.reshape(processor_total, place_limit, term_count)...  7.33 us
    dynamic_update_slice x4, local copies, waits for them, and re-layouts, contract_cost_tile(): lax.dynamic_update_index_in_dim(valued_contracts, contract_worths, cost_t...  2.92 us
  transfers between devices with their start and end apart: 2, of which 2 were waited for; matrix products, arithmetic and copies ran while one was open for 0% of the time, Pallas kernels for 0%

profile of v1, /device:TPU:0, one launch (start us, length us, event | category | flops | bytes accessed | tf_op | source)
XLA Modules:
  0.0 139.6 jit_solution(1773420543230276039)
XLA Ops:
  0.6 0.0 copy-start.1
  0.6 0.7 copy-done.1
  1.3 0.1 fusion.14
  1.5 0.3 reduce_window_sum.11
  1.7 0.2 select_reduce_fusion
  2.0 2.6 %scatter_custom_fusion = f32[256,1024]{1,0:T(8,128)} fusion(s32[128]{0:T(128)S(1)} %fusion.15, f32[128,1024]{1,0:T(8,128)} %param.11, f32[]{:T(128)} %constant.174.clone.1), kind=kCustom, calls=%fused_computation.23 | custom fusion | bytes 1049088 | tf_op jit(solution)/shard_map/scatter | solution.py:61
  4.6 7.3 %all-to-all-start = ((f32[32,8,1024]{2,1,0:T(8,128)}), f32[32,8,1024]{2,1,0:T(8,128)S(1)}, u32[]{:S(2)}, u32[]{:S(2)}) async-start(f32[32,8,1024]{2,1,0:T(8,128)} %bitcast.11), calls=%async_computation | async-start | bytes 2097152 | tf_op jit(solution)/shard_map/all_to_all | solution.py:62
  11.9 27.5 %all-to-all-done = f32[32,8,1024]{2,1,0:T(8,128)S(1)} async-done(((f32[32,8,1024]{2,1,0:T(8,128)}), f32[32,8,1024]{2,1,0:T(8,128)S(1)}, u32[]{:S(2)}, u32[]{:S(2)}) %all-to-all-start) | async-done | bytes 1048608 | tf_op jit(solution)/shard_map/all_to_all | solution.py:62
  39.4 24.5 %while.15 = (s32[]{:T(128)}, f32[4,8,4,8,256]{4,3,2,1,0:T(8,128)}, f32[1,1024]{1,0:T(1,128)}, f32[1,1024]{1,0:T(1,128)}, f32[4,8,8,1024]{3,2,1,0:T(8,128)S(1)}, ...) while((s32[]{:T(128)}, f32[4,8,4,8,256]{4,3,2,1,0:T(8,128)}, f32[1,1024]{1,0:T(1,128)}, ...), condition=%wide.region_4.5_spmd, body=%wide.region_3.4_spmd.sunk | while | flops 806621696 | bytes 1858191 | solution.py:88
  39.4 0.7 dynamic-slice_add_fusion.2
  40.1 4.7 %convolution_bitcast_fusion.4 = f32[1,8,4,8,256]{4,3,1,2,0:T(8,128)S(1)} fusion(f32[4,8,8,1024]{3,2,1,0:T(8,128)S(1)} %get-tuple-element.222, f32[256]{0:T(256)S(1)} %bitcast.62, f32[1024]{0:T(1024)S(1)} %get-tuple-element.197, f32[256]{0:T(256)S(1)} %bitcast.63, f32[1024]{0:T(1024)S(1)} %get-tuple-element.199), kind=kOutput, calls=%fused_computation.2.clone.1 | convolution fusion | flops 806617088 | bytes 1320960 | tf_op jit(solution)/shard_map/while/body/eval_jaxpr/abmk,sk->bams/dot_general | solution.py:81
  44.8 0.7 copy_dynamic-update-slice_fusion.2
  45.5 0.7 dynamic-slice_add_fusion.2
  46.2 4.7 %convolution_bitcast_fusion.4 = f32[1,8,4,8,256]{4,3,1,2,0:T(8,128)S(1)} fusion(f32[4,8,8,1024]{3,2,1,0:T(8,128)S(1)} %get-tuple-element.222, f32[256]{0:T(256)S(1)} %bitcast.62, f32[1024]{0:T(1024)S(1)} %get-tuple-element.197, f32[256]{0:T(256)S(1)} %bitcast.63, f32[1024]{0:T(1024)S(1)} %get-tuple-element.199), kind=kOutput, calls=%fused_computation.2.clone.1 | convolution fusion | flops 806617088 | bytes 1320960 | tf_op jit(solution)/shard_map/while/body/eval_jaxpr/abmk,sk->bams/dot_general | solution.py:81
  50.9 0.7 copy_dynamic-update-slice_fusion.2
  51.6 0.7 dynamic-slice_add_fusion.2
  52.3 4.7 %convolution_bitcast_fusion.4 = f32[1,8,4,8,256]{4,3,1,2,0:T(8,128)S(1)} fusion(f32[4,8,8,1024]{3,2,1,0:T(8,128)S(1)} %get-tuple-element.222, f32[256]{0:T(256)S(1)} %bitcast.62, f32[1024]{0:T(1024)S(1)} %get-tuple-element.197, f32[256]{0:T(256)S(1)} %bitcast.63, f32[1024]{0:T(1024)S(1)} %get-tuple-element.199), kind=kOutput, calls=%fused_computation.2.clone.1 | convolution fusion | flops 806617088 | bytes 1320960 | tf_op jit(solution)/shard_map/while/body/eval_jaxpr/abmk,sk->bams/dot_general | solution.py:81
  57.0 0.7 copy_dynamic-update-slice_fusion.2
  57.7 0.7 dynamic-slice_add_fusion.2
  58.5 4.7 %convolution_bitcast_fusion.4 = f32[1,8,4,8,256]{4,3,1,2,0:T(8,128)S(1)} fusion(f32[4,8,8,1024]{3,2,1,0:T(8,128)S(1)} %get-tuple-element.222, f32[256]{0:T(256)S(1)} %bitcast.62, f32[1024]{0:T(1024)S(1)} %get-tuple-element.197, f32[256]{0:T(256)S(1)} %bitcast.63, f32[1024]{0:T(1024)S(1)} %get-tuple-element.199), kind=kOutput, calls=%fused_computation.2.clone.1 | convolution fusion | flops 806617088 | bytes 1320960 | tf_op jit(solution)/shard_map/while/body/eval_jaxpr/abmk,sk->bams/dot_general | solution.py:81
  63.1 0.7 copy_dynamic-update-slice_fusion.2
  63.9 0.0 copy-start.2
  63.9 2.8 %all-to-all-start.1 = ((f32[32,4,8,256]{3,2,1,0:T(8,128)}), f32[32,4,8,256]{3,2,1,0:T(8,128)S(1)}, u32[]{:S(2)}, u32[]{:S(2)}) async-start(f32[32,4,8,256]{3,2,1,0:T(8,128)} %bitcast.13), calls=%async_computation.1 | async-start | bytes 2097152 | tf_op jit(solution)/shard_map/all_to_all | solution.py:91
  66.7 0.0 copy-done.2
  66.7 0.6 reduce_sum.50
  68.0 26.2 %all-to-all-done.1 = f32[32,4,8,256]{3,2,1,0:T(8,128)S(1)} async-done(((f32[32,4,8,256]{3,2,1,0:T(8,128)}), f32[32,4,8,256]{3,2,1,0:T(8,128)S(1)}, u32[]{:S(2)}, u32[]{:S(2)}) %all-to-all-start.1) | async-done | bytes 1048608 | tf_op jit(solution)/shard_map/all_to_all | solution.py:91
  94.1 1.6 %gather_fusion = f32[512,256]{1,0:T(8,128)S(1)} fusion(f32[1024,256]{1,0:T(8,128)S(1)} %bitcast.60, s32[1024]{0:T(1024)S(1)} %pad_clamp_fusion), kind=kCustom, calls=%fused_computation | custom fusion | bytes 1050624 | tf_op jit(solution)/shard_map/jit(_take)/gather | solution.py:101
  95.7 0.1 broadcast_select_fusion
  95.9 0.0 copy-start
  95.9 0.5 fusion.17
  96.4 0.0 copy-start.3
  96.4 0.0 copy-start.4
  96.4 8.7 %all-reduce.1 = (f32[512]{0:T(512)S(1)}, f32[]{:T(128)}) all-reduce(f32[512]{0:T(512)S(1)} %bitcast.71, f32[]{:T(128)} %reduce_sum.50), channel_id=1, replica_groups=mesh['scen'=4,'opt'=8] {'scen'}, use_global_device_ids=true, to_apply=%region_5.6 | all-reduce | flops 513 | bytes 4104 | tf_op jit(solution)/shard_map/psum | solution.py:114
  105.1 0.0 copy-done.3
  105.1 0.0 copy-done.4
  105.1 0.3 convolution_bitcast_fusion.2
  105.4 10.3 %all-gather.2 = f32[8,1,256]{2,1,0:T(1,128)S(1)} all-gather(f32[1,1,256]{2,1,0:T(1,128)S(1)} %convolution_bitcast_fusion.2), channel_id=2, replica_groups=mesh['scen'=4,'opt'=8] {'opt'}, dimensions={0}, use_global_device_ids=true | all-gather | bytes 9216 | tf_op jit(solution)/shard_map/all_gather | solution.py:17
  116.4 0.0 copy-start.5
  116.4 0.7 copy-done.5
  117.0 0.6 fusion.16
  117.6 0.5 fusion.18
  118.2 8.6 %all-reduce = (f32[512]{0:T(512)S(1)}, f32[]{:T(128)}) all-reduce(f32[512]{0:T(512)S(1)} %bitcast.70, f32[]{:T(128)} %get-tuple-element.153), channel_id=1, replica_groups=mesh['scen'=4,'opt'=8] {'scen'}, use_global_device_ids=true, to_apply=%region_9.10 | all-reduce | flops 513 | bytes 4104 | tf_op jit(solution)/shard_map/psum | solution.py:114
  127.4 0.6 multiply_subtract_fusion
  128.0 0.0 copy-done
  128.0 0.3 convolution_bitcast_fusion.1
  128.3 9.6 %all-gather.3 = f32[8,1,256]{2,1,0:T(1,128)S(1)} all-gather(f32[1,1,256]{2,1,0:T(1,128)S(1)} %convolution_bitcast_fusion.1), channel_id=3, replica_groups=mesh['scen'=4,'opt'=8] {'opt'}, dimensions={0}, use_global_device_ids=true | all-gather | bytes 9216 | tf_op jit(solution)/shard_map/all_gather | solution.py:17
  137.9 0.6 add_clamp_fusion
  (12 shorter events, 0.1 us)
Async XLA Ops:
  0.6 0.7 copy-start.1
  4.6 34.8 %all-to-all-start = ((f32[32,8,1024]{2,1,0:T(8,128)}), f32[32,8,1024]{2,1,0:T(8,128)S(1)}, u32[]{:S(2)}, u32[]{:S(2)}) async-start(f32[32,8,1024]{2,1,0:T(8,128)} %bitcast.11), calls=%async_computation | async-start | bytes 2097152 | tf_op jit(solution)/shard_map/all_to_all | solution.py:62
  63.9 2.8 %copy-start.2 = (f32[256]{0:T(256)S(1)}, f32[256]{0:T(256)}, u32[]{:S(2)}) copy-start(f32[256]{0:T(256)} %param.18) | copy-start | bytes 3076
  63.9 30.3 %all-to-all-start.1 = ((f32[32,4,8,256]{3,2,1,0:T(8,128)}), f32[32,4,8,256]{3,2,1,0:T(8,128)S(1)}, u32[]{:S(2)}, u32[]{:S(2)}) async-start(f32[32,4,8,256]{3,2,1,0:T(8,128)} %bitcast.13), calls=%async_computation.1 | async-start | bytes 2097152 | tf_op jit(solution)/shard_map/all_to_all | solution.py:91
  95.9 32.2 %copy-start = (f32[512,256]{1,0:T(8,128)}, f32[512,256]{1,0:T(8,128)S(1)}, u32[]{:S(2)}) copy-start(f32[512,256]{1,0:T(8,128)S(1)} %broadcast_select_fusion) | copy-start | bytes 1572868
  96.4 8.7 %copy-start.3 = (f32[512]{0:T(512)S(1)}, f32[512]{0:T(512)}, u32[]{:S(2)}) copy-start(f32[512]{0:T(512)} %param.16) | copy-start | bytes 6148
  96.4 8.7 %copy-start.4 = (f32[512]{0:T(512)S(1)}, f32[512]{0:T(512)}, u32[]{:S(2)}) copy-start(f32[512]{0:T(512)} %param.15) | copy-start | bytes 6148
  116.4 0.7 copy-start.5
